TPU v7x, 256 devices: a whole 4x4x8 slice. The times are simulated.
256 devices in a mesh: snap: 8 (over y, core), vtx: 32 (over z, x).
Axes of the slice: x: 4, y: 4, z: 8, core: 2. Of those that a mesh axis runs over, the one named last changes fastest.
Arguments:
- features: bfloat16 [16, 32768, 128], P('snap', 'vtx'), may hold values from -6 to 6
- tile_vals: bfloat16 [16, 256, 16, 128, 128], P('snap', 'vtx'), may hold values from -0.25 to 0.25
- tile_cols: int32 [16, 256, 16], P('snap', 'vtx'), may hold values from 0 to 255, as said below
- tile_count: int32 [16, 256], P('snap', 'vtx'), may hold values from 1 to 16
- gcn_weight: bfloat16 [128, 128], replicated, may hold values from -0.5 to 0.5
- gcn_bias: float32 [128], replicated, may hold values from -3 to 3
- input_weight: bfloat16 [128, 512], replicated, may hold values from -0.5 to 0.5
- recur_weight: bfloat16 [128, 512], replicated, may hold values from -0.5 to 0.5
- lstm_bias: float32 [512], replicated, may hold values from -4 to 4
- hidden_grad: bfloat16 [32, 1024, 16, 128], P('vtx', 'snap'), may hold values from -6 to 6
Outputs:
- hidden_states: bfloat16 [32, 1024, 16, 128], P('vtx', 'snap')
- grad_gcn_weight: float32 [128, 128], replicated
- grad_gcn_bias: float32 [128], replicated
- grad_input_weight: float32 [128, 512], replicated
- grad_recur_weight: float32 [128, 512], replicated
- grad_lstm_bias: float32 [512], replicated
Inputs may be any that keep to these rules, and one draw needn't show every extreme that they name: `tile_cols`: within one snapshot, the 16 slots of one row block name distinct column blocks, and all slots, live or not, of the row blocks j * 8 to (j + 1) * 8 - 1 together name at most one block of each group of 8 consecutive blocks.
All inputs are finite; a program needn't handle non-finite values.
Results may differ from a plain program's by a relative error of at most 0.0085.
Values may be sent and summed in bfloat16 or wider, within the bound.
No kernel may reach another device: no remote copies, remote signals or barrier semaphores. Data moves between devices by JAX's collectives and lax.ppermute only.
A program may use at most 128 MiB of HBM per device.

v0:
```python
import jax
import jax.numpy as jnp
from jax import lax
from jax.sharding import PartitionSpec as P


def silu_slope(grad_layer, pre_act):
    squeeze = jax.nn.sigmoid(pre_act)
    return (grad_layer.astype(jnp.float32) * squeeze * (1.0 + pre_act * (1.0 - squeeze))).astype(
        jnp.bfloat16
    )


def on_device(
    features,
    tile_vals,
    tile_cols,
    tile_count,
    gcn_weight,
    gcn_bias,
    input_weight,
    recur_weight,
    lstm_bias,
    hidden_grad,
):
    steps_dev, local_verts, feat_width = features.shape
    tile_size = tile_vals.shape[3]
    hidden_size = recur_weight.shape[0]
    live_mask = lax.broadcasted_iota(jnp.int32, tile_cols.shape, 2) < tile_count[:, :, None]
    snap_iota = lax.broadcasted_iota(jnp.int32, tile_cols.shape, 0)
    gathered = lax.all_gather(features, "vtx", axis=1, tiled=True)
    whole_blocks = gathered.reshape(steps_dev, -1, tile_size, feat_width)
    fetched_blocks = whole_blocks[snap_iota, tile_cols]
    blocks_used = jnp.where(
        live_mask[..., None, None], fetched_blocks, jnp.zeros_like(fetched_blocks)
    )
    summed = jnp.einsum(
        "svmij,svmjf->svif", tile_vals, blocks_used, preferred_element_type=jnp.float32
    )
    aggregated = summed.astype(jnp.bfloat16).reshape(steps_dev * local_verts, feat_width)
    pre_act = jnp.dot(aggregated, gcn_weight, preferred_element_type=jnp.float32) + gcn_bias
    layer_out = (
        jax.nn.silu(pre_act).astype(jnp.bfloat16).reshape(steps_dev, local_verts, feat_width)
    )
    vertex_inputs = lax.all_to_all(layer_out, "snap", split_axis=1, concat_axis=0, tiled=True)
    total_steps, vertex_rows, _ = vertex_inputs.shape
    flat_inputs = vertex_inputs.reshape(total_steps * vertex_rows, feat_width)
    input_gates = (
        jnp.dot(flat_inputs, input_weight, preferred_element_type=jnp.float32) + lstm_bias
    ).reshape(total_steps, vertex_rows, 4 * hidden_size)

    def advance(carried, gates_step):
        cell_state, last_out = carried
        pre_gates = gates_step + jnp.dot(last_out, recur_weight, preferred_element_type=jnp.float32)
        gate_in = jax.nn.sigmoid(pre_gates[:, :hidden_size])
        gate_keep = jax.nn.sigmoid(pre_gates[:, hidden_size : 2 * hidden_size])
        gate_new = jnp.tanh(pre_gates[:, 2 * hidden_size : 3 * hidden_size])
        gate_out = jax.nn.sigmoid(pre_gates[:, 3 * hidden_size :])
        cell_state = gate_keep * cell_state + gate_in * gate_new
        new_out = (gate_out * jnp.tanh(cell_state)).astype(jnp.bfloat16)
        return ((cell_state, new_out), (pre_gates, cell_state, new_out))

    zero_cell = jnp.zeros((vertex_rows, hidden_size), jnp.float32)
    start = (zero_cell, jnp.zeros((vertex_rows, hidden_size), jnp.bfloat16))
    _, (all_pre, all_cells, all_outs) = lax.scan(advance, start, input_gates)
    prev_cells = jnp.concatenate([zero_cell[None], all_cells[:-1]], axis=0)
    prev_outs = jnp.concatenate([start[1][None], all_outs[:-1]], axis=0)
    grad_outs = jnp.transpose(hidden_grad[0], (1, 0, 2)).astype(jnp.float32)

    def retreat(carried, step_items):
        grad_cell, grad_back = carried
        pre_gates, cell_state, prev_cell, grad_out = step_items
        gate_in = jax.nn.sigmoid(pre_gates[:, :hidden_size])
        gate_keep = jax.nn.sigmoid(pre_gates[:, hidden_size : 2 * hidden_size])
        gate_new = jnp.tanh(pre_gates[:, 2 * hidden_size : 3 * hidden_size])
        gate_out = jax.nn.sigmoid(pre_gates[:, 3 * hidden_size :])
        squash = jnp.tanh(cell_state)
        grad_total = grad_out + grad_back
        grad_cell = grad_cell + grad_total * gate_out * (1.0 - squash * squash)
        grad_gates = jnp.concatenate(
            [
                grad_cell * gate_new * gate_in * (1.0 - gate_in),
                grad_cell * prev_cell * gate_keep * (1.0 - gate_keep),
                grad_cell * gate_in * (1.0 - gate_new * gate_new),
                grad_total * squash * gate_out * (1.0 - gate_out),
            ],
            axis=1,
        ).astype(jnp.bfloat16)
        grad_back = jnp.einsum(
            "rg,hg->rh", grad_gates, recur_weight, preferred_element_type=jnp.float32
        )
        return ((grad_cell * gate_keep, grad_back), grad_gates)

    _, all_grad_gates = lax.scan(
        retreat, (zero_cell, zero_cell), (all_pre, all_cells, prev_cells, grad_outs), reverse=True
    )
    flat_gates = all_grad_gates.reshape(total_steps * vertex_rows, 4 * hidden_size)
    grad_input = jnp.einsum(
        "rf,rg->fg", flat_inputs, flat_gates, preferred_element_type=jnp.float32
    )
    grad_recur = jnp.einsum(
        "rh,rg->hg",
        prev_outs.reshape(total_steps * vertex_rows, hidden_size),
        flat_gates,
        preferred_element_type=jnp.float32,
    )
    grad_bias = jnp.sum(flat_gates.astype(jnp.float32), axis=0)
    grad_layer = jnp.einsum(
        "rg,fg->rf", flat_gates, input_weight, preferred_element_type=jnp.float32
    ).astype(jnp.bfloat16)
    grad_snap = lax.all_to_all(
        grad_layer.reshape(total_steps, vertex_rows, feat_width),
        "snap",
        split_axis=0,
        concat_axis=1,
        tiled=True,
    )
    grad_snap = grad_snap.reshape(steps_dev * local_verts, feat_width)
    grad_pre = silu_slope(grad_snap, pre_act)
    grad_gcn = jnp.einsum("rf,rg->fg", aggregated, grad_pre, preferred_element_type=jnp.float32)
    grad_gbias = jnp.sum(grad_pre.astype(jnp.float32), axis=0)
    grad_gcn, grad_gbias, grad_input, grad_recur, grad_bias = lax.psum(
        (grad_gcn, grad_gbias, grad_input, grad_recur, grad_bias), ("snap", "vtx")
    )
    hidden_states = jnp.transpose(all_outs, (1, 0, 2))[None]
    return (hidden_states, grad_gcn, grad_gbias, grad_input, grad_recur, grad_bias)


def solution(mesh):
    return jax.shard_map(
        on_device,
        mesh=mesh,
        in_specs=(
            P("snap", "vtx", None),
            P("snap", "vtx", None, None, None),
            P("snap", "vtx", None),
            P("snap", "vtx"),
            P(),
            P(),
            P(),
            P(),
            P(),
            P("vtx", "snap", None, None),
        ),
        out_specs=(P("vtx", "snap", None, None), P(), P(), P(), P(), P()),
        check_vma=False,
    )
```

profile of v0, /device:TPU:1, one launch (start us, length us, event | category | flops | bytes accessed | tf_op | source)
XLA Modules:
  0.0 570.2 jit_solution(6579747021246747212)
XLA Ops:
  9.5 145.1 %all-gather.2.cloned.1.call-done = bf16[2,32768,128]{2,1,0:T(8,128)(2,1)} async-done(((bf16[2,1024,128]{2,1,0:T(8,128)(2,1)}), bf16[2,32768,128]{2,1,0:T(8,128)(2,1)}) %all-gather.2.cloned.1.call-update) | async-done | bytes 16777232 | tf_op jit(solution)/shard_map/all_gather | solution.py:31
  154.6 15.9 %gather_fusion = bf16[256,128,128]{2,1,0:T(8,128)(2,1)} fusion(bf16[2,256,128,128]{3,2,1,0:T(8,128)(2,1)} %bitcast.136, s32[256]{0:T(256)S(1)} %reshape.144), kind=kCustom, calls=%fused_computation | custom fusion | bytes 16779264 | tf_op jit(solution)/shard_map/gather | solution.py:33
  170.4 8.2 %fusion.53 = bf16[2,8,128,128]{2,3,1,0:T(8,128)(2,1)S(1)} fusion(bf16[2,8,16,128,128]{4,3,2,1,0:T(8,128)(2,1)} %param.15, bf16[2,8,16,128,128]{4,3,2,1,0:T(8,128)(2,1)} %bitcast.132, pred[2,8,16]{2,1,0:T(8,128)(4,1)S(1)} %iota_compare_fusion), kind=kOutput, calls=%fused_computation.77 | convolution fusion | flops 1078198272 | bytes 17301760 | tf_op jit(solution)/shard_map/svmij,svmjf->svif/dot_general | solution.py:37
  182.2 5.3 all-to-all-start
  188.6 8.3 %all-to-all-done = bf16[2,1024,128]{2,0,1:T(2,128)(2,1)S(1)} async-done(((bf16[2,1024,128]{2,0,1:T(2,128)(2,1)}), bf16[2,1024,128]{2,0,1:T(2,128)(2,1)S(1)}, u32[]{:S(2)}, u32[]{:S(2)}) %all-to-all-start) | async-done | bytes 524320 | tf_op jit(solution)/shard_map/all_to_all | solution.py:45
  197.1 2.6 convolution_add_fusion.1
  199.7 41.2 %while.38 = (s32[]{:T(128)}, f32[128,128]{1,0:T(8,128)S(1)}, bf16[128,128]{1,0:T(8,128)(2,1)S(1)}, f32[16,128,512]{2,1,0:T(8,128)}, f32[16,128,128]{2,1,0:T(8,12...) while((s32[]{:T(128)}, f32[128,128]{1,0:T(8,128)S(1)}, ...), condition=%wide.region_1.2_spmd.clone, body=%wide.region_0.1_spmd.clone.sunk | while | flops 17104900 | bytes 1541236 | solution.py:65
  199.7 1.9 bitcast_dynamic-update-slice_fusion.6
  202.3 1.8 bitcast_dynamic-update-slice_fusion.6
  204.9 1.9 bitcast_dynamic-update-slice_fusion.6
  210.0 1.8 bitcast_dynamic-update-slice_fusion.6
  220.3 1.9 bitcast_dynamic-update-slice_fusion.6
  225.5 1.8 bitcast_dynamic-update-slice_fusion.6
  228.0 1.8 bitcast_dynamic-update-slice_fusion.6
  233.2 1.8 bitcast_dynamic-update-slice_fusion.6
  235.7 1.9 bitcast_dynamic-update-slice_fusion.6
  238.3 1.9 bitcast_dynamic-update-slice_fusion.6
  242.5 49.4 %while.39 = (s32[]{:T(128)}, f32[128,128]{1,0:T(8,128)S(1)}, f32[128,128]{1,0:T(8,128)S(1)}, bf16[16,128,512]{2,1,0:T(8,128)(2,1)S(1)}, f32[16,128,128]{2,1,0:T(...) while((s32[]{:T(128)}, f32[128,128]{1,0:T(8,128)S(1)}, ...), condition=%wide.region_3.4_spmd.clone, body=%wide.region_2.3_spmd.clone.sunk | while | flops 18481156 | bytes 2162843 | solution.py:94
  291.9 2.1 copy.34
  295.5 4.3 all-to-all-start.1
  299.8 2.2 convolution_bitcast_fusion
  303.1 6.1 %all-to-all-done.1 = bf16[16,128,128]{2,1,0:T(8,128)(2,1)S(1)} async-done(((bf16[16,128,128]{2,1,0:T(8,128)(2,1)}), bf16[16,128,128]{2,1,0:T(8,128)(2,1)S(1)}, u32[]{:S(2)}, u32[]{:S(2)}) %all-to-all-start.1) | async-done | bytes 524320 | tf_op jit(solution)/shard_map/all_to_all | solution.py:111
  313.4 73.9 %all-reduce.2 = (f32[128]{0:T(128)}, f32[512]{0:T(512)}) all-reduce(f32[128]{0:T(128)S(1)} %get-tuple-element.334, f32[512]{0:T(512)S(1)} %convert_reduce_fusion), channel_id=1, replica_groups=mesh['snap'=8,'vtx'=32] {'snap','vtx'}, use_global_device_ids=true, to_apply=%region_6.7 | all-reduce | flops 640 | bytes 5120 | tf_op jit(solution)/shard_map/psum | solution.py:122
  387.4 171.2 %all-reduce.6.cloned.1.call-done = (f32[128,128]{1,0:T(8,128)}, f32[128,512]{1,0:T(8,128)}, f32[128,512]{1,0:T(8,128)}) async-done(((f32[128,128]{1,0:T(8,128)}, f32[128,512]{1,0:T(8,128)}, f32[128,512]{1,0:T(8,128)}), (f32[128,128]{1,0:T(8,128)}, f32[128,512]{1,0:T(8,128)}, f32[128,512]{1,0:T(8,128)})) %all-reduce.6.cloned.1.call-update) | async-done | bytes 589840 | tf_op jit(solution)/shard_map/psum | solution.py:122
  (173 shorter events, 91.3 us)
Async XLA Ops:
  7.2 189.9 %copy-start = (bf16[128,512]{1,0:T(8,128)(2,1)S(1)}, bf16[128,512]{1,0:T(8,128)(2,1)}, u32[]{:S(2)}) copy-start(bf16[128,512]{1,0:T(8,128)(2,1)} %param.20) | copy-start | bytes 393220
  7.2 147.4 %all-gather.2.cloned.1.call-start = ((), (), s32[]{:S(2)}) async-start(), calls=%async_computation.2 | async-start | bytes 17301504 | tf_op jit(solution)/shard_map/all_gather | solution.py:31
  170.4 9.0 %copy-start.9 = (bf16[128,128]{1,0:T(8,128)(2,1)S(1)}, bf16[128,128]{1,0:T(8,128)(2,1)}, u32[]{:S(2)}) copy-start(bf16[128,128]{1,0:T(8,128)(2,1)} %param.18) | copy-start | bytes 98308
  170.4 9.0 %copy-start.10 = (f32[128]{0:T(128)S(1)}, f32[128]{0:T(128)}, u32[]{:S(2)}) copy-start(f32[128]{0:T(128)} %param.19) | copy-start | bytes 1540
  178.6 0.8 copy-start.6
  178.6 8.9 %copy-start.5 = (bf16[1,128,16,128]{3,2,1,0:T(8,128)(2,1)S(1)}, bf16[1,128,16,128]{3,2,1,0:T(8,128)(2,1)}, u32[]{:S(2)}) copy-start(bf16[1,128,16,128]{3,2,1,0:T(8,128)(2,1)} %param.23) | copy-start | bytes 1572868
  180.8 16.3 %copy-start.8 = (f32[512]{0:T(512)S(1)}, f32[512]{0:T(512)}, u32[]{:S(2)}) copy-start(f32[512]{0:T(512)} %param.22) | copy-start | bytes 6148
  182.2 14.8 %all-to-all-start = ((bf16[2,1024,128]{2,0,1:T(2,128)(2,1)}), bf16[2,1024,128]{2,0,1:T(2,128)(2,1)S(1)}, u32[]{:S(2)}, u32[]{:S(2)}) async-start(bf16[2,1024,128]{2,0,1:T(2,128)(2,1)} %copy.28), calls=%async_computation | async-start | bytes 1048576 | tf_op jit(solution)/shard_map/all_to_all | solution.py:45
  187.5 12.2 %copy-start.1 = (bf16[128,512]{1,0:T(8,128)(2,1)S(1)}, bf16[128,512]{1,0:T(8,128)(2,1)}, u32[]{:S(2)}) copy-start(bf16[128,512]{1,0:T(8,128)(2,1)} %param.21) | copy-start | bytes 393220
  240.9 1.3 copy-start.3
  295.5 13.8 %all-to-all-start.1 = ((bf16[16,128,128]{2,1,0:T(8,128)(2,1)}), bf16[16,128,128]{2,1,0:T(8,128)(2,1)S(1)}, u32[]{:S(2)}, u32[]{:S(2)}) async-start(bf16[16,128,128]{2,1,0:T(8,128)(2,1)} %bitcast.143), calls=%async_computation.1 | async-start | bytes 1048576 | tf_op jit(solution)/shard_map/all_to_all | solution.py:111
  299.8 258.8 %all-reduce.6.cloned.1.call-start = ((), (), s32[]{:S(2)}) async-start(), calls=%async_computation.3 | async-start | bytes 1179648 | tf_op jit(solution)/shard_map/psum | solution.py:122
  303.1 8.8 %copy-start.2 = (bf16[16,128,128]{2,1,0:T(8,128)(2,1)S(1)}, bf16[16,128,128]{2,1,0:T(8,128)(2,1)}, u32[]{:S(2)}) copy-start(bf16[16,128,128]{2,1,0:T(8,128)(2,1)} %get-tuple-element.229) | copy-start | bytes 1572868
  309.3 1.2 copy-start.4
  309.3 1.7 copy-start.7
Sparse Core Ops, SparseCore 0:
  10.6 143.9 all-gather.1
  312.1 246.4 all-reduce.5
where the time goes:
time: 573 us; the launch traced here: 570 us
  waiting for transfers between devices  331 us (58%)
  blocking collectives  73.9 us (13%)
  matrix products  50.5 us (9%)
  other arithmetic  44.9 us (8%)
  local copies, waits for them, and re-layouts  44.5 us (8%)
  between operations  14.2 us (2%)
  starting transfers between devices  9.64 us (2%)
    psum x1, waiting for transfers between devices, on_device(): lax.psum((grad_gcn, grad_gbias, grad_input, grad_recur, grad_bias), ('sna...  171 us
    all_gather x1, waiting for transfers between devices, on_device(): gathered = lax.all_gather(features, 'vtx', axis=1, tiled=True)  145 us
    psum x1, blocking collectives, on_device(): lax.psum((grad_gcn, grad_gbias, grad_input, grad_recur, grad_bias), ('sna...  73.9 us
    another operation x32, other arithmetic  29.8 us
    dot_general x16, matrix products, advance(): jnp.dot(last_out, recur_weight, preferred_element_type=jnp.float32)  29.5 us
    gather x1, local copies, waits for them, and re-layouts, on_device(): fetched_blocks = whole_blocks[snap_iota, tile_cols]  15.9 us
    squeeze x16, local copies, waits for them, and re-layouts, on_device(): _, (all_pre, all_cells, all_outs) = lax.scan(advance, start, input_gates)  15.6 us
  transfers between devices with their start and end apart: 4, of which 4 were waited for; matrix products, arithmetic and copies ran while one was open for 1% of the time, Pallas kernels for 0%

commit v1 on v0

--- a/solution.py
+++ b/solution.py
@@ -28,7 +28,9 @@
     hidden_size = recur_weight.shape[0]
     live_mask = lax.broadcasted_iota(jnp.int32, tile_cols.shape, 2) < tile_count[:, :, None]
     snap_iota = lax.broadcasted_iota(jnp.int32, tile_cols.shape, 0)
-    gathered = lax.all_gather(features, "vtx", axis=1, tiled=True)
+    gathered = jnp.concatenate(
+        lax.all_to_all(jnp.stack([features] * lax.axis_size("vtx")), "vtx", 0, 0), axis=1
+    )
     whole_blocks = gathered.reshape(steps_dev, -1, tile_size, feat_width)
     fetched_blocks = whole_blocks[snap_iota, tile_cols]
     blocks_used = jnp.where(

time: 573 us -> 856 us (1.49)
  waiting for transfers between devices: 331 us -> 569 us
  local copies, waits for them, and re-layouts: 44.5 us -> 65.4 us
  blocking collectives: 73.9 us -> 87.5 us
  starting transfers between devices: 9.64 us -> 22.3 us
    all_to_all x0 -> x1, waiting for transfers between devices: none -> 383 us  [on_device(): lax.all_to_all(jnp.stack([features] * lax.axis_size('vtx')), 'vtx', 0, 0)]
    all_gather x1 -> x0, waiting for transfers between devices: 145 us -> none  [on_device(): gathered = lax.all_gather(features, 'vtx', axis=1, tiled=True)]
    all_to_all x0 -> x1, local copies, waits for them, and re-layouts: none -> 13.8 us  [on_device(): lax.all_to_all(jnp.stack([features] * lax.axis_size('vtx')), 'vtx', 0, 0)]
    psum x1, blocking collectives: 73.9 us -> 87.5 us  [on_device(): lax.psum((grad_gcn, grad_gbias, grad_input, grad_recur, grad_bias), ('sna...]
    all_to_all x0 -> x1, starting transfers between devices: none -> 12.1 us  [on_device(): lax.all_to_all(jnp.stack([features] * lax.axis_size('vtx')), 'vtx', 0, 0)]
where the time goes in v1:
time: 856 us; the launch traced here: 853 us
  waiting for transfers between devices  569 us (66%)
  blocking collectives  87.5 us (10%)
  local copies, waits for them, and re-layouts  65.4 us (8%)
  matrix products  50.4 us (6%)
  other arithmetic  43.6 us (5%)
  starting transfers between devices  22.3 us (3%)
  between operations  14.2 us (2%)
    all_to_all x1, waiting for transfers between devices, on_device(): lax.all_to_all(jnp.stack([features] * lax.axis_size('vtx')), 'vtx', 0, 0)  383 us
    psum x1, waiting for transfers between devices, on_device(): lax.psum((grad_gcn, grad_gbias, grad_input, grad_recur, grad_bias), ('sna...  171 us
    psum x1, blocking collectives, on_device(): lax.psum((grad_gcn, grad_gbias, grad_input, grad_recur, grad_bias), ('sna...  87.5 us
    another operation x32, other arithmetic  29.8 us
    dot_general x16, matrix products, advance(): jnp.dot(last_out, recur_weight, preferred_element_type=jnp.float32)  29.4 us
  transfers between devices with their start and end apart: 4, of which 4 were waited for; matrix products, arithmetic and copies ran while one was open for 1% of the time, Pallas kernels for 0%

profile of v1, /device:TPU:1, one launch (start us, length us, event | category | flops | bytes accessed | tf_op | source)
XLA Modules:
  0.0 852.9 jit_solution(12356946114949138079)
XLA Ops:
  7.2 7.0 stack.2
  14.2 12.1 %all-to-all-start = ((bf16[32,2,1024,128]{3,2,1,0:T(8,128)(2,1)}), bf16[32,2,1024,128]{3,2,1,0:T(8,128)(2,1)}, u32[]{:S(2)}, u32[]{:S(2)}) async-start(bf16[32,2,1024,128]{3,2,1,0:T(8,128)(2,1)} %stack.2), calls=%async_computation | async-start | bytes 33554432 | tf_op jit(solution)/shard_map/all_to_all | solution.py:32
  26.5 382.9 %all-to-all-done = bf16[32,2,1024,128]{3,2,1,0:T(8,128)(2,1)} async-done(((bf16[32,2,1024,128]{3,2,1,0:T(8,128)(2,1)}), bf16[32,2,1024,128]{3,2,1,0:T(8,128)(2,1)}, u32[]{:S(2)}, u32[]{:S(2)}) %all-to-all-start) | async-done | bytes 16777248 | tf_op jit(solution)/shard_map/all_to_all | solution.py:32
  409.4 13.8 %copy.28 = bf16[32,2,1024,128]{3,2,0,1:T(8,128)(2,1)} copy(bf16[32,2,1024,128]{3,2,1,0:T(8,128)(2,1)} %all-to-all-done) | data formatting | bytes 33554432 | tf_op jit(solution)/shard_map/all_to_all | solution.py:32
  423.2 15.9 %gather_fusion = bf16[256,128,128]{2,1,0:T(8,128)(2,1)} fusion(bf16[2,256,128,128]{3,2,1,0:T(8,128)(2,1)} %bitcast.134, s32[256]{0:T(256)S(1)} %reshape.146), kind=kCustom, calls=%fused_computation | custom fusion | bytes 16779264 | tf_op jit(solution)/shard_map/gather | solution.py:35
  439.1 8.2 fusion.53
  450.9 5.9 all-to-all-start.1
  457.9 8.3 all-to-all-done.1
  466.4 2.6 convolution_add_fusion.1
  469.0 41.1 %while.38 = (s32[]{:T(128)}, f32[128,128]{1,0:T(8,128)S(1)}, bf16[128,128]{1,0:T(8,128)(2,1)S(1)}, f32[16,128,512]{2,1,0:T(8,128)}, f32[16,128,128]{2,1,0:T(8,12...) while((s32[]{:T(128)}, f32[128,128]{1,0:T(8,128)S(1)}, ...), condition=%wide.region_1.2_spmd.clone, body=%wide.region_0.1_spmd.clone.sunk | while | flops 17104900 | bytes 1541236 | solution.py:67
  469.0 1.8 bitcast_dynamic-update-slice_fusion.6
  471.6 1.8 bitcast_dynamic-update-slice_fusion.6
  474.2 1.8 bitcast_dynamic-update-slice_fusion.6
  489.5 1.8 bitcast_dynamic-update-slice_fusion.6
  494.7 1.8 bitcast_dynamic-update-slice_fusion.6
  504.9 1.9 bitcast_dynamic-update-slice_fusion.6
  507.5 1.9 bitcast_dynamic-update-slice_fusion.6
  511.6 49.4 %while.39 = (s32[]{:T(128)}, f32[128,128]{1,0:T(8,128)S(1)}, f32[128,128]{1,0:T(8,128)S(1)}, bf16[16,128,512]{2,1,0:T(8,128)(2,1)S(1)}, f32[16,128,128]{2,1,0:T(...) while((s32[]{:T(128)}, f32[128,128]{1,0:T(8,128)S(1)}, ...), condition=%wide.region_3.4_spmd.clone, body=%wide.region_2.3_spmd.clone.sunk | while | flops 18481156 | bytes 2162843 | solution.py:96
  561.1 2.1 copy.35
  564.7 4.3 all-to-all-start.2
  568.9 2.2 convolution_bitcast_fusion
  572.3 6.1 all-to-all-done.2
  582.6 87.5 %all-reduce.2 = (f32[128]{0:T(128)}, f32[512]{0:T(512)}) all-reduce(f32[128]{0:T(128)S(1)} %get-tuple-element.334, f32[512]{0:T(512)S(1)} %convert_reduce_fusion), channel_id=1, replica_groups=mesh['snap'=8,'vtx'=32] {'snap','vtx'}, use_global_device_ids=true, to_apply=%region_6.7 | all-reduce | flops 640 | bytes 5120 | tf_op jit(solution)/shard_map/psum | solution.py:124
  670.1 171.2 %all-reduce.6.cloned.1.call-done = (f32[128,128]{1,0:T(8,128)}, f32[128,512]{1,0:T(8,128)}, f32[128,512]{1,0:T(8,128)}) async-done(((f32[128,128]{1,0:T(8,128)}, f32[128,512]{1,0:T(8,128)}, f32[128,512]{1,0:T(8,128)}), (f32[128,128]{1,0:T(8,128)}, f32[128,512]{1,0:T(8,128)}, f32[128,512]{1,0:T(8,128)})) %all-reduce.6.cloned.1.call-update) | async-done | bytes 589840 | tf_op jit(solution)/shard_map/psum | solution.py:124
  (178 shorter events, 94.7 us)
Async XLA Ops:
  7.2 459.2 %copy-start = (bf16[128,512]{1,0:T(8,128)(2,1)S(1)}, bf16[128,512]{1,0:T(8,128)(2,1)}, u32[]{:S(2)}) copy-start(bf16[128,512]{1,0:T(8,128)(2,1)} %param.20) | copy-start | bytes 393220
  14.2 12.1 %copy-start.8 = (s32[2,8,16]{2,1,0:T(8,128)S(1)}, s32[2,8,16]{2,1,0:T(8,128)}, u32[]{:S(2)}) copy-start(s32[2,8,16]{2,1,0:T(8,128)} %param.16) | copy-start | bytes 3076
  14.2 12.2 %copy-start.10 = (s32[2,8]{1,0:T(2,128)S(1)}, s32[2,8]{1,0:T(2,128)}, u32[]{:S(2)}) copy-start(s32[2,8]{1,0:T(2,128)} %param.17) | copy-start | bytes 196
  14.2 395.2 %all-to-all-start = ((bf16[32,2,1024,128]{3,2,1,0:T(8,128)(2,1)}), bf16[32,2,1024,128]{3,2,1,0:T(8,128)(2,1)}, u32[]{:S(2)}, u32[]{:S(2)}) async-start(bf16[32,2,1024,128]{3,2,1,0:T(8,128)(2,1)} %stack.2), calls=%async_computation | async-start | bytes 33554432 | tf_op jit(solution)/shard_map/all_to_all | solution.py:32
  439.1 9.0 %copy-start.11 = (bf16[128,128]{1,0:T(8,128)(2,1)S(1)}, bf16[128,128]{1,0:T(8,128)(2,1)}, u32[]{:S(2)}) copy-start(bf16[128,128]{1,0:T(8,128)(2,1)} %param.18) | copy-start | bytes 98308
  439.1 9.0 %copy-start.12 = (f32[128]{0:T(128)S(1)}, f32[128]{0:T(128)}, u32[]{:S(2)}) copy-start(f32[128]{0:T(128)} %param.19) | copy-start | bytes 1540
  447.3 0.8 copy-start.6
  447.3 9.5 %copy-start.5 = (bf16[1,128,16,128]{3,2,1,0:T(8,128)(2,1)S(1)}, bf16[1,128,16,128]{3,2,1,0:T(8,128)(2,1)}, u32[]{:S(2)}) copy-start(bf16[1,128,16,128]{3,2,1,0:T(8,128)(2,1)} %param.23) | copy-start | bytes 1572868
  449.5 16.9 %copy-start.9 = (f32[512]{0:T(512)S(1)}, f32[512]{0:T(512)}, u32[]{:S(2)}) copy-start(f32[512]{0:T(512)} %param.22) | copy-start | bytes 6148
  450.9 15.4 %all-to-all-start.1 = ((bf16[2,1024,128]{2,0,1:T(2,128)(2,1)}), bf16[2,1024,128]{2,0,1:T(2,128)(2,1)S(1)}, u32[]{:S(2)}, u32[]{:S(2)}) async-start(bf16[2,1024,128]{2,0,1:T(2,128)(2,1)} %copy.29), calls=%async_computation.1 | async-start | bytes 1048576 | tf_op jit(solution)/shard_map/all_to_all | solution.py:47
  456.8 12.2 %copy-start.1 = (bf16[128,512]{1,0:T(8,128)(2,1)S(1)}, bf16[128,512]{1,0:T(8,128)(2,1)}, u32[]{:S(2)}) copy-start(bf16[128,512]{1,0:T(8,128)(2,1)} %param.21) | copy-start | bytes 393220
  510.1 1.3 copy-start.3
  564.7 13.8 %all-to-all-start.2 = ((bf16[16,128,128]{2,1,0:T(8,128)(2,1)}), bf16[16,128,128]{2,1,0:T(8,128)(2,1)S(1)}, u32[]{:S(2)}, u32[]{:S(2)}) async-start(bf16[16,128,128]{2,1,0:T(8,128)(2,1)} %bitcast.145), calls=%async_computation.2 | async-start | bytes 1048576 | tf_op jit(solution)/shard_map/all_to_all | solution.py:113
  568.9 272.3 %all-reduce.6.cloned.1.call-start = ((), (), s32[]{:S(2)}) async-start(), calls=%async_computation.3 | async-start | bytes 1179648 | tf_op jit(solution)/shard_map/psum | solution.py:124
  572.3 8.8 %copy-start.2 = (bf16[16,128,128]{2,1,0:T(8,128)(2,1)S(1)}, bf16[16,128,128]{2,1,0:T(8,128)(2,1)}, u32[]{:S(2)}) copy-start(bf16[16,128,128]{2,1,0:T(8,128)(2,1)} %get-tuple-element.229) | copy-start | bytes 1572868
  578.4 1.2 copy-start.4
  578.4 1.7 copy-start.7
Sparse Core Ops, SparseCore 0:
  581.2 260.0 all-reduce.5
